TPU v7x, 32 devices: a whole 2x2x4 slice. The times are simulated.
32 devices in a mesh: ctx: 8 (over y, x, core), ch: 4 (over z).
Axes of the slice: x: 2, y: 2, z: 4, core: 2. Of those that a mesh axis runs over, the one named last changes fastest.
Arguments:
- query_act: bfloat16 [4096, 4096], P('ctx', 'ch'), may hold values from -6 to 6
- key_act: bfloat16 [4096, 4096], P('ctx', 'ch'), may hold values from -6 to 6
- value_act: bfloat16 [4096, 4096], P('ctx', 'ch'), may hold values from -6 to 6
- filters: bfloat16 [4096, 128], P('ch'), may hold values from -0.5 to 0.5
- proj_weight: bfloat16 [8192, 4096], P('ctx', 'ch'), may hold values from -0.09375 to 0.09375
- cotangent: bfloat16 [4096, 8192], P('ctx', 'ch'), may hold values from -6 to 6
Outputs:
- grad_query: bfloat16 [4096, 4096], P('ctx', 'ch')
- grad_key: bfloat16 [4096, 4096], P('ctx', 'ch')
- grad_value: bfloat16 [4096, 4096], P('ctx', 'ch')
- grad_filter: float32 [4096, 128], P('ch')
- grad_proj: float32 [8192, 4096], P('ctx', 'ch')
All inputs are finite; a program needn't handle non-finite values.
Results may differ from a plain program's by a relative error of at most 0.0051.
Values may be sent and summed in bfloat16 or wider, within the bound.
A program may use at most 192 MiB of HBM per device.

v0:
```python
import jax
import jax.numpy as jnp
import numpy as np
from jax import lax
from jax.sharding import PartitionSpec as P

TAPS = 128


def from_behind(x, axis, by):
    length = lax.axis_size(axis)
    pairs = [(i, i + by) for i in range(length) if 0 <= i + by < length]
    return lax.ppermute(x, axis, pairs)


def basis(points):
    freqs = points // 2
    phase = (2 * np.arange(freqs)[:, None] + 1) * np.arange(points)[None, :] % (2 * points)
    angle = np.pi * phase / points
    return np.concatenate([np.cos(angle), np.sin(angle)], 0).astype(np.float32)


def split(a):
    a = jnp.asarray(a, jnp.float32)
    hi = a.astype(jnp.bfloat16)
    return (hi, (a - hi.astype(jnp.float32)).astype(jnp.bfloat16))


def dot32(a, b):
    return jnp.dot(a, b, preferred_element_type=jnp.float32)


def forward(table, x):
    hi, lo = split(table)
    return dot32(hi, x) + dot32(lo, x)


def backward(table, y):
    thi, tlo = split(table)
    yhi, ylo = split(y)
    return dot32(thi, yhi) + dot32(thi, ylo) + dot32(tlo, yhi)


def halves(x):
    n = x.shape[0] // 2
    return (x[:n], x[n:])


def times(x, f):
    (xc, xs), (fc, fs) = (halves(x), halves(f))
    return jnp.concatenate([xc * fc - xs * fs, xc * fs + xs * fc], 0)


def times_conj(x, f):
    (xc, xs), (fc, fs) = (halves(x), halves(f))
    return jnp.concatenate([xc * fc + xs * fs, xs * fc - xc * fs], 0)


def shards(query_act, key_act, value_act, filters, proj_weight, cotangent):
    tokens = query_act.shape[0]
    points = tokens + TAPS
    table = basis(points)
    inverse = (table.T / (points // 2)).astype(np.float32)
    gathered = lax.all_gather(cotangent, "ch", axis=1, tiled=True)
    weight = lax.all_gather(proj_weight, "ctx", axis=0, tiled=True)
    query_f = query_act.astype(jnp.float32)
    key_f = key_act.astype(jnp.float32)
    value_f = value_act.astype(jnp.float32)
    product = (key_f * value_f).astype(jnp.bfloat16)
    before = from_behind(product[tokens - TAPS :], "ctx", 1)
    filt_spec = forward(table[:, :TAPS], filters.T)
    prod_spec = forward(table[:, :TAPS], before) + forward(table[:, TAPS:], product)
    mixed = backward(inverse[TAPS:], times(prod_spec, filt_spec))
    gated = (query_f * mixed).astype(jnp.bfloat16)
    partial_grad = lax.dot_general(
        gathered, gated, (((0,), (0,)), ((), ())), preferred_element_type=jnp.float32
    ).astype(jnp.bfloat16)
    grad_proj = lax.psum_scatter(partial_grad, "ctx", scatter_dimension=0, tiled=True).astype(
        jnp.float32
    )
    grad_mix = dot32(gathered, weight)
    grad_query = (grad_mix * mixed).astype(jnp.bfloat16)
    grad_gate = (grad_mix * query_f).astype(jnp.bfloat16)
    after = from_behind(grad_gate[:TAPS], "ctx", -1)
    own_spec = forward(table[:, :tokens], grad_gate)
    gate_spec = own_spec + forward(table[:, tokens:], after)
    lags = inverse[TAPS - np.arange(TAPS)]
    local_filter = backward(lags, times_conj(prod_spec, own_spec))
    grad_filter = lax.psum(local_filter, "ctx").T
    grad_prod = backward(inverse[:tokens], times_conj(gate_spec, filt_spec))
    grad_key = (grad_prod * value_f).astype(jnp.bfloat16)
    grad_value = (grad_prod * key_f).astype(jnp.bfloat16)
    return (grad_query, grad_key, grad_value, grad_filter, grad_proj)


def solution(mesh):
    return jax.shard_map(
        shards,
        mesh=mesh,
        in_specs=(
            P("ctx", "ch"),
            P("ctx", "ch"),
            P("ctx", "ch"),
            P("ch", None),
            P("ctx", "ch"),
            P("ctx", "ch"),
        ),
        out_specs=(P("ctx", "ch"), P("ctx", "ch"), P("ctx", "ch"), P("ch", None), P("ctx", "ch")),
        check_vma=False,
    )
```

profile of v0, /device:TPU:0, one launch (start us, length us, event | category | flops | bytes accessed | tf_op | source)
XLA Modules:
  0.0 497.0 jit_solution(8108205557831197759)
XLA Ops:
  8.8 1.3 copy.19
  10.1 1.3 copy.20
  12.4 149.5 %all-gather.3.cloned.1.call-done = bf16[512,8192]{1,0:T(8,128)(2,1)} async-done(((bf16[512,2048]{1,0:T(8,128)(2,1)}), bf16[512,8192]{1,0:T(8,128)(2,1)}) %all-gather.3.cloned.1.call-update) | async-done | bytes 8388624 | tf_op jit(solution)/shard_map/all_gather | solution.py:64
  162.0 90.0 %all-gather.5.cloned.1.call-done = bf16[8192,1024]{1,0:T(8,128)(2,1)} async-done(((bf16[1024,1024]{1,0:T(8,128)(2,1)}), bf16[8192,1024]{1,0:T(8,128)(2,1)}) %all-gather.5.cloned.1.call-update) | async-done | bytes 16777232 | tf_op jit(solution)/shard_map/all_gather | solution.py:65
  251.9 14.9 %fusion.6 = (bf16[512,1024]{1,0:T(8,128)(2,1)S(1)}, f32[512,1024]{1,0:T(8,128)S(1)}) fusion(bf16[512,1024]{1,0:T(8,128)(2,1)} %param.14, bf16[512,8192]{1,0:T(8,128)(2,1)} %all-gather.3.cloned.1.call-done, bf16[8192,1024]{1,0:T(8,128)(2,1)} %all-gather.5.cloned.1.call-done), kind=kOutput, calls=%fused_computation.20 | convolution fusion | flops 8591507456 | bytes 29360128 | tf_op jit(solution)/shard_map/dot_general | solution.py:30
  266.9 1.4 collective-permute-start.1
  272.6 1.0 fusion.8
  273.7 1.0 fusion.21
  275.4 2.7 fusion.3
  278.1 6.7 %collective-permute-start = (bf16[128,1024]{0,1:T(8,128)(2,1)S(1)}, bf16[128,1024]{0,1:T(8,128)(2,1)S(1)}, u32[]{:S(2)}, u32[]{:S(2)}) collective-permute-start(bf16[128,1024]{0,1:T(8,128)(2,1)S(1)} %slice.44), channel_id=1, source_target_pairs={{0,4},{4,8},{8,12},{12,16},{16,20},{20,24},{24,28},{1,5},{5,9},{9,... | collective-permute-start | bytes 786440 | tf_op jit(solution)/shard_map/ppermute | solution.py:13
  285.7 0.9 fusion.37
  288.2 2.5 multiply_add_fusion
  290.7 1.0 fusion.14
  291.8 1.0 fusion.17
  292.8 2.1 multiply_convert_fusion
  294.9 15.9 %convert_bitcast_fusion = bf16[8192,1024]{0,1:T(8,128)(2,1)} fusion(bf16[512,8192]{1,0:T(8,128)(2,1)} %all-gather.3.cloned.1.call-done, f32[512,1024]{1,0:T(8,128)S(1)} %get-tuple-element.24, bf16[512,1024]{1,0:T(8,128)(2,1)S(1)} %copy-done.25), kind=kOutput, calls=%fused_computation | convolution fusion | flops 8599896064 | bytes 28311552 | tf_op jit(solution)/shard_map/dot_general | solution.py:75
  311.0 1.0 copy-done.2
  313.9 1.4 fusion.12
  315.4 2.4 copy.26
  317.7 1.3 copy.25
  319.0 111.5 %reduce-scatter.2.cloned.1.call-done = bf16[1024,1024]{0,1:T(8,128)(2,1)} async-done(((bf16[8192,1024]{0,1:T(8,128)(2,1)}), bf16[1024,1024]{0,1:T(8,128)(2,1)}) %reduce-scatter.2.cloned.1.call-update) | async-done | bytes 2097168 | tf_op jit(solution)/shard_map/reduce_scatter | solution.py:78
  430.5 4.2 copy.27
  434.6 53.9 %all-reduce.2.cloned.1.call-done = f32[1024,128]{1,0:T(8,128)} async-done(((f32[1024,128]{1,0:T(8,128)}), f32[1024,128]{1,0:T(8,128)}) %all-reduce.2.cloned.1.call-update) | async-done | bytes 524304 | tf_op jit(solution)/shard_map/psum | solution.py:89
  488.6 1.9 copy.33
  (75 shorter events, 12.2 us)
Async XLA Ops:
  7.2 4.2 copy-start
  7.2 1.6 copy-start.10
  7.2 154.8 %all-gather.3.cloned.1.call-start = ((), (), s32[]{:S(2)}) async-start(), calls=%async_computation.1 | async-start | bytes 10485760 | tf_op jit(solution)/shard_map/all_gather | solution.py:64
  7.9 2.2 copy-start.11
  7.9 244.0 %all-gather.5.cloned.1.call-start = ((), (), s32[]{:S(2)}) async-start(), calls=%async_computation.2 | async-start | bytes 18874368 | tf_op jit(solution)/shard_map/all_gather | solution.py:65
  8.7 2.7 copy-start.20
  8.7 421.8 %reduce-scatter.2.cloned.1.call-start = ((), (), s32[]{:S(2)}) async-start(), calls=%async_computation.4 | async-start | bytes 18874368 | tf_op jit(solution)/shard_map/reduce_scatter | solution.py:78
  10.1 1.8 copy-start.13
  12.4 255.9 %copy-start.9 = (bf16[640,512]{1,0:T(8,128)(2,1)S(1)}, bf16[640,512]{1,0:T(8,128)(2,1)}, u32[]{:S(2)}) copy-start(bf16[640,512]{1,0:T(8,128)(2,1)} %constant.33) | copy-start | bytes 1966084
  266.9 2.3 copy-start.18
  266.9 3.6 collective-permute-start.1
  273.7 1.5 copy-start.6
  273.7 1.7 copy-start.12
  275.4 9.4 %copy-start.17 = (bf16[640,512]{1,0:T(8,128)(2,1)S(1)}, bf16[640,512]{1,0:T(8,128)(2,1)}, u32[]{:S(2)}) copy-start(bf16[640,512]{1,0:T(8,128)(2,1)} %constant.28) | copy-start | bytes 1966084
  278.1 7.6 %copy-start.16 = (bf16[640,512]{1,0:T(8,128)(2,1)S(1)}, bf16[640,512]{1,0:T(8,128)(2,1)}, u32[]{:S(2)}) copy-start(bf16[640,512]{1,0:T(8,128)(2,1)} %constant.25) | copy-start | bytes 1966084
  278.1 8.5 %collective-permute-start = (bf16[128,1024]{0,1:T(8,128)(2,1)S(1)}, bf16[128,1024]{0,1:T(8,128)(2,1)S(1)}, u32[]{:S(2)}, u32[]{:S(2)}) collective-permute-start(bf16[128,1024]{0,1:T(8,128)(2,1)S(1)} %slice.44), channel_id=1, source_target_pairs={{0,4},{4,8},{8,12},{12,16},{16,20},{20,24},{24,28},{1,5},{5,9},{9,... | collective-permute-start | bytes 786440 | tf_op jit(solution)/shard_map/ppermute | solution.py:13
  288.2 2.5 copy-start.15
  292.7 2.1 copy-start.25
  310.7 1.3 copy-start.2
  310.7 1.7 copy-start.3
  310.7 1.7 copy-start.19
  310.8 177.8 %all-reduce.2.cloned.1.call-start = ((), (), s32[]{:S(2)}) async-start(), calls=%async_computation.3 | async-start | bytes 1048576 | tf_op jit(solution)/shard_map/psum | solution.py:89
  315.3 2.4 copy-start.4
  430.5 60.0 %copy-start.1 = (bf16[1024,128]{1,0:T(8,128)(2,1)S(1)}, bf16[1024,128]{1,0:T(8,128)(2,1)}, u32[]{:S(2)}) copy-start(bf16[1024,128]{1,0:T(8,128)(2,1)} %param.17) | copy-start | bytes 786436
  (8 other events, 8.3 us)
Sparse Core Ops, SparseCore 0:
  9.6 152.3 all-gather.2
  163.9 88.0 all-gather.4
  310.9 119.5 reduce-scatter.1
  434.0 54.5 all-reduce.1
where the time goes:
time: 498 us; the launch traced here: 497 us
  waiting for transfers between devices  407 us (82%)
  matrix products  48.7 us (10%)
  local copies, waits for them, and re-layouts  15.9 us (3%)
  between operations  14.1 us (3%)
  starting transfers between devices  8.5 us (2%)
    all_gather x1, waiting for transfers between devices, shards(): gathered = lax.all_gather(cotangent, 'ch', axis=1, tiled=True)  150 us
    reduce_scatter x1, waiting for transfers between devices, shards(): lax.psum_scatter(partial_grad, 'ctx', scatter_dimension=0, tiled=True)  111 us
    all_gather x1, waiting for transfers between devices, shards(): weight = lax.all_gather(proj_weight, 'ctx', axis=0, tiled=True)  90 us
    psum x1, waiting for transfers between devices, shards(): grad_filter = lax.psum(local_filter, 'ctx').T  53.9 us
    dot_general x20, matrix products, dot32(): return jnp.dot(a, b, preferred_element_type=jnp.float32)  32.9 us
    dot_general x1, matrix products, shards(): lax.dot_general(gathered, gated, (((0,), (0,)), ((), ())), preferred_elem...  15.9 us
    unnamed x58, local copies, waits for them, and re-layouts  15.9 us
  transfers between devices with their start and end apart: 6, of which 5 were waited for; matrix products, arithmetic and copies ran while one was open for 4% of the time, Pallas kernels for 0%

commit v1 on v0

--- a/solution.py
+++ b/solution.py
@@ -3,8 +3,15 @@
 import numpy as np
 from jax import lax
 from jax.sharding import PartitionSpec as P
+from jax.lax import axis_index, axis_size, ppermute
 
 TAPS = 128
+
+
+def post_the_clusters(original, dim_k):
+    all_rows = list(original.shape[1:])
+    all_rows[dim_k] *= original.shape[0]
+    return jnp.moveaxis(original, 0, dim_k).reshape(all_rows)
 
 
 def from_behind(x, axis, by):
@@ -62,7 +69,23 @@
     table = basis(points)
     inverse = (table.T / (points // 2)).astype(np.float32)
     gathered = lax.all_gather(cotangent, "ch", axis=1, tiled=True)
-    weight = lax.all_gather(proj_weight, "ctx", axis=0, tiled=True)
+    count_all = axis_size("ctx")
+    queue = tuple(((jj, (jj + 1) % count_all) for jj in range(count_all)))
+    line_up = tuple(((src_i, num) for num, src_i in queue))
+    plain, passed = ([], [])
+    rr = 0
+    while rr < count_all - 1:
+        if rr % 2 == 0:
+            plain.append(ppermute(plain[-1] if plain else proj_weight, axis_name="ctx", perm=queue))
+        else:
+            passed.append(
+                ppermute(passed[-1] if passed else proj_weight, axis_name="ctx", perm=line_up)
+            )
+        rr = rr + 1
+    found_now = jnp.stack([*plain[::-1], proj_weight, *passed], 0)
+    inter = axis_index("ctx") - len(plain)
+    found_now = found_now[(jnp.arange(count_all) - inter) % count_all]
+    weight = post_the_clusters(found_now, 0)
     query_f = query_act.astype(jnp.float32)
     key_f = key_act.astype(jnp.float32)
     value_f = value_act.astype(jnp.float32)

time: 498 us -> 470 us (0.944)
  waiting for transfers between devices: 407 us -> 325 us
  local copies, waits for them, and re-layouts: 15.9 us -> 53.8 us
  other arithmetic: 3.06 us -> 16.7 us
    ppermute x0 -> x7, waiting for transfers between devices: none -> 153 us  [the longest x4 153 us: shards(): ppermute(plain[-1] if plain else proj_weight, axis_name='ctx', perm=queue)]
    all_gather x1, waiting for transfers between devices: 150 us -> 0.01 us  [shards(): gathered = lax.all_gather(cotangent, 'ch', axis=1, tiled=True)]
    all_gather x1 -> x0, waiting for transfers between devices: 90 us -> none  [shards(): weight = lax.all_gather(proj_weight, 'ctx', axis=0, tiled=True)]
    gather x0 -> x3, local copies, waits for them, and re-layouts: none -> 22.4 us  [shards(): found_now = found_now[(jnp.arange(count_all) - inter) % count_all]]
    unnamed x58 -> x75, local copies, waits for them, and re-layouts: 15.9 us -> 31.1 us
    unnamed x0 -> x1, other arithmetic: none -> 13.7 us
    ppermute x0 -> x7, starting transfers between devices: none -> 7.24 us  [the longest x3 6.73 us: shards(): ppermute(passed[-1] if passed else proj_weight, axis_name='ctx', perm=lin...]
  transfers between devices with their start and end apart: 6 -> 12, of which waited for: 5 -> 7; matrix products, arithmetic and copies ran while one was open for 4% -> 14% of each run, Pallas kernels for 0% -> 0%
where the time goes in v1:
time: 470 us; the launch traced here: 469 us
  waiting for transfers between devices  325 us (69%)
  local copies, waits for them, and re-layouts  53.8 us (11%)
  matrix products  48.5 us (10%)
  other arithmetic  16.7 us (4%)
  between operations  14.2 us (3%)
  starting transfers between devices  11.5 us (2%)
    ppermute x4, waiting for transfers between devices, shards(): ppermute(plain[-1] if plain else proj_weight, axis_name='ctx', perm=queue)  153 us
    reduce_scatter x1, waiting for transfers between devices, shards(): lax.psum_scatter(partial_grad, 'ctx', scatter_dimension=0, tiled=True)  116 us
    psum x1, waiting for transfers between devices, shards(): grad_filter = lax.psum(local_filter, 'ctx').T  54.1 us
    dot_general x20, matrix products, dot32(): return jnp.dot(a, b, preferred_element_type=jnp.float32)  33.4 us
    unnamed x75, local copies, waits for them, and re-layouts  31.1 us
    gather x3, local copies, waits for them, and re-layouts, shards(): found_now = found_now[(jnp.arange(count_all) - inter) % count_all]  22.4 us
    dot_general x1, matrix products, shards(): lax.dot_general(gathered, gated, (((0,), (0,)), ((), ())), preferred_elem...  15.1 us
    unnamed x1, other arithmetic  13.7 us
  transfers between devices with their start and end apart: 12, of which 7 were waited for; matrix products, arithmetic and copies ran while one was open for 14% of the time, Pallas kernels for 0%

profile of v1, /device:TPU:0, one launch (start us, length us, event | category | flops | bytes accessed | tf_op | source)
XLA Modules:
  0.0 469.4 jit_solution(17967071979211600506)
XLA Ops:
  8.0 26.7 %collective-permute-done = bf16[1024,1024]{1,0:T(8,128)(2,1)} collective-permute-done((bf16[1024,1024]{1,0:T(8,128)(2,1)}, bf16[1024,1024]{1,0:T(8,128)(2,1)}, u32[]{:S(2)}, u32[]{:S(2)}) %collective-permute-start) | collective-permute-done | bytes 2097184 | tf_op jit(solution)/shard_map/ppermute | solution.py:79
  34.7 2.6 collective-permute-start.4
  37.3 44.8 %collective-permute-done.1 = bf16[1024,1024]{1,0:T(8,128)(2,1)S(1)} collective-permute-done((bf16[1024,1024]{1,0:T(8,128)(2,1)}, bf16[1024,1024]{1,0:T(8,128)(2,1)S(1)}, u32[]{:S(2)}, u32[]{:S(2)}) %collective-permute-start.1) | collective-permute-done | bytes 2097184 | tf_op jit(solution)/shard_map/ppermute | solution.py:79
  84.9 44.9 %collective-permute-done.2 = bf16[1024,1024]{1,0:T(8,128)(2,1)} collective-permute-done((bf16[1024,1024]{1,0:T(8,128)(2,1)S(1)}, bf16[1024,1024]{1,0:T(8,128)(2,1)}, u32[]{:S(2)}, u32[]{:S(2)}) %collective-permute-start.2) | collective-permute-done | bytes 2097184 | tf_op jit(solution)/shard_map/ppermute | solution.py:79
  129.8 2.4 copy.22
  135.9 2.7 collective-permute-start.6
  138.6 36.9 %collective-permute-done.3 = bf16[1024,1024]{1,0:T(8,128)(2,1)} collective-permute-done((bf16[1024,1024]{1,0:T(8,128)(2,1)}, bf16[1024,1024]{1,0:T(8,128)(2,1)}, u32[]{:S(2)}, u32[]{:S(2)}) %collective-permute-start.3) | collective-permute-done | bytes 2097184 | tf_op jit(solution)/shard_map/ppermute | solution.py:79
  177.3 1.9 bitcast_dynamic-update-slice_fusion.6
  179.7 1.9 bitcast_dynamic-update-slice_fusion.4
  185.8 6.3 %fusion.39 = (bf16[8,512,1024]{2,1,0:T(8,128)(2,1)}, bf16[8,512,1024]{2,1,0:T(8,128)(2,1)}) fusion(bf16[8,1024,1024]{2,1,0:T(8,128)(2,1)S(1)} %bitcast_dynamic-update-slice_fusion), kind=kLoop, calls=%fused_computation.71 | loop fusion | bytes 33554432 | tf_op jit(solution)/shard_map/gather | solution.py:87
  192.1 8.1 %gather_fusion = bf16[8,512,1024]{2,1,0:T(8,128)(2,1)} fusion(bf16[8,512,1024]{2,1,0:T(8,128)(2,1)} %get-tuple-element.10, s32[1024]{0:T(1024)S(1)} %pad_clamp_fusion), kind=kCustom, calls=%fused_computation | custom fusion | bytes 16777248 | tf_op jit(solution)/shard_map/gather | solution.py:87
  200.2 8.1 %gather_fusion.1 = bf16[8,512,1024]{2,1,0:T(8,128)(2,1)} fusion(bf16[8,512,1024]{2,1,0:T(8,128)(2,1)} %get-tuple-element.11, s32[1024]{0:T(1024)S(1)} %pad_clamp_fusion), kind=kCustom, calls=%fused_computation.1 | custom fusion | bytes 16777248 | tf_op jit(solution)/shard_map/gather | solution.py:87
  208.3 13.7 %pad_maximum_fusion = bf16[8,1024,1024]{2,1,0:T(8,128)(2,1)} fusion(bf16[8,512,1024]{2,1,0:T(8,128)(2,1)} %gather_fusion.1, bf16[8,512,1024]{2,1,0:T(8,128)(2,1)} %gather_fusion), kind=kLoop, calls=%fused_computation.2 | loop fusion | flops 33554432 | bytes 33554432
  221.9 15.1 %fusion.6 = (bf16[512,1024]{0,1:T(8,128)(2,1)S(1)}, f32[1024,512]{1,0:T(8,128)S(1)}) fusion(bf16[512,1024]{0,1:T(8,128)(2,1)} %copy.22, bf16[8192,1024]{1,0:T(8,128)(2,1)} %bitcast.66, bf16[512,8192]{1,0:T(8,128)(2,1)} %all-gather.2.cloned.1.call-done), kind=kOutput, calls=%fused_computation.23 | convolution fusion | flops 8591507456 | bytes 29360128 | tf_op jit(solution)/shard_map/dot_general | solution.py:37
  246.5 2.7 fusion.3
  249.3 2.6 collective-permute-start.7
  255.3 2.4 multiply_add_fusion
  259.8 2.1 fusion.8
  262.0 15.1 %convert_bitcast_fusion = bf16[8192,1024]{0,1:T(8,128)(2,1)} fusion(bf16[512,8192]{1,0:T(8,128)(2,1)} %all-gather.2.cloned.1.call-done, f32[512,1024]{0,1:T(8,128)S(1)} %get-tuple-element.26, bf16[512,1024]{0,1:T(8,128)(2,1)S(1)} %copy-done.16), kind=kOutput, calls=%fused_computation.3 | convolution fusion | flops 8599896064 | bytes 28311552 | tf_op jit(solution)/shard_map/dot_general | solution.py:98
  281.7 2.4 copy.26
  286.7 116.1 %reduce-scatter.2.cloned.1.call-done = bf16[1024,1024]{0,1:T(8,128)(2,1)} async-done(((bf16[8192,1024]{0,1:T(8,128)(2,1)}), bf16[1024,1024]{0,1:T(8,128)(2,1)}) %reduce-scatter.2.cloned.1.call-update) | async-done | bytes 2097168 | tf_op jit(solution)/shard_map/reduce_scatter | solution.py:101
  402.8 4.2 copy.28
  406.9 54.1 %all-reduce.2.cloned.1.call-done = f32[1024,128]{1,0:T(8,128)} async-done(((f32[1024,128]{1,0:T(8,128)}), f32[1024,128]{1,0:T(8,128)}) %all-reduce.2.cloned.1.call-update) | async-done | bytes 524304 | tf_op jit(solution)/shard_map/psum | solution.py:112
  461.0 1.9 copy.40
  (110 shorter events, 35.6 us)
Async XLA Ops:
  7.2 127.7 %copy-start = (bf16[1024,128]{1,0:T(8,128)(2,1)S(1)}, bf16[1024,128]{1,0:T(8,128)(2,1)}, u32[]{:S(2)}) copy-start(bf16[1024,128]{1,0:T(8,128)(2,1)} %param.17) | copy-start | bytes 786436
  7.2 27.5 %copy-start.10 = (bf16[1024,1024]{1,0:T(8,128)(2,1)S(1)}, bf16[1024,1024]{1,0:T(8,128)(2,1)}, u32[]{:S(2)}) copy-start(bf16[1024,1024]{1,0:T(8,128)(2,1)} %param.18) | copy-start | bytes 6291460
  7.2 125.0 %copy-start.14 = (bf16[512,1024]{1,0:T(8,128)(2,1)S(1)}, bf16[512,1024]{1,0:T(8,128)(2,1)}, u32[]{:S(2)}) copy-start(bf16[512,1024]{1,0:T(8,128)(2,1)} %param.15) | copy-start | bytes 3145732
  7.2 214.7 %all-gather.2.cloned.1.call-start = ((), (), s32[]{:S(2)}) async-start(), calls=%async_computation.1 | async-start | bytes 10485760 | tf_op jit(solution)/shard_map/all_gather | solution.py:71
  7.2 27.4 %collective-permute-start = (bf16[1024,1024]{1,0:T(8,128)(2,1)}, bf16[1024,1024]{1,0:T(8,128)(2,1)}, u32[]{:S(2)}, u32[]{:S(2)}) collective-permute-start(bf16[1024,1024]{1,0:T(8,128)(2,1)} %param.18), channel_id=1, source_target_pairs={{0,4},{4,8},{8,12},{12,16},{16,20},{20,24},{24,28},{28,0},{1,5},{5... | collective-permute-start | bytes 6291464 | tf_op jit(solution)/shard_map/ppermute | solution.py:79
  7.9 394.9 %reduce-scatter.2.cloned.1.call-start = ((), (), s32[]{:S(2)}) async-start(), calls=%async_computation.3 | async-start | bytes 18874368 | tf_op jit(solution)/shard_map/reduce_scatter | solution.py:101
  34.7 47.5 %collective-permute-start.1 = (bf16[1024,1024]{1,0:T(8,128)(2,1)}, bf16[1024,1024]{1,0:T(8,128)(2,1)S(1)}, u32[]{:S(2)}, u32[]{:S(2)}) collective-permute-start(bf16[1024,1024]{1,0:T(8,128)(2,1)} %collective-permute-done), channel_id=1, source_target_pairs={{0,4},{4,8},{8,12},{12,16},{16,20},{20,24},{24,28},{28,0},{1,5},{5... | collective-permute-start | bytes 6291464 | tf_op jit(solution)/shard_map/ppermute | solution.py:79
  34.7 47.5 %collective-permute-start.4 = (bf16[1024,1024]{1,0:T(8,128)(2,1)S(1)}, bf16[1024,1024]{1,0:T(8,128)(2,1)}, u32[]{:S(2)}, u32[]{:S(2)}) collective-permute-start(bf16[1024,1024]{1,0:T(8,128)(2,1)S(1)} %copy-done.10), channel_id=1, source_target_pairs={{4,0},{8,4},{12,8},{16,12},{20,16},{24,20},{28,24},{0,28},{5,1},{9... | collective-permute-start | bytes 6291464 | tf_op jit(solution)/shard_map/ppermute | solution.py:82
  82.2 47.6 %collective-permute-start.2 = (bf16[1024,1024]{1,0:T(8,128)(2,1)S(1)}, bf16[1024,1024]{1,0:T(8,128)(2,1)}, u32[]{:S(2)}, u32[]{:S(2)}) collective-permute-start(bf16[1024,1024]{1,0:T(8,128)(2,1)S(1)} %collective-permute-done.1), channel_id=1, source_target_pairs={{0,4},{4,8},{8,12},{12,16},{16,20},{20,24},{24,28},{28,0},{1,5},{5... | collective-permute-start | bytes 6291464 | tf_op jit(solution)/shard_map/ppermute | solution.py:79
  83.5 52.4 %collective-permute-start.5 = (bf16[1024,1024]{1,0:T(8,128)(2,1)}, bf16[1024,1024]{1,0:T(8,128)(2,1)}, u32[]{:S(2)}, u32[]{:S(2)}) collective-permute-start(bf16[1024,1024]{1,0:T(8,128)(2,1)} %collective-permute-done.4), channel_id=1, source_target_pairs={{4,0},{8,4},{12,8},{16,12},{20,16},{24,20},{28,24},{0,28},{5,1},{9... | collective-permute-start | bytes 6291464 | tf_op jit(solution)/shard_map/ppermute | solution.py:82
  129.8 45.7 %collective-permute-start.3 = (bf16[1024,1024]{1,0:T(8,128)(2,1)}, bf16[1024,1024]{1,0:T(8,128)(2,1)}, u32[]{:S(2)}, u32[]{:S(2)}) collective-permute-start(bf16[1024,1024]{1,0:T(8,128)(2,1)} %collective-permute-done.2), channel_id=1, source_target_pairs={{0,4},{4,8},{8,12},{12,16},{16,20},{20,24},{24,28},{28,0},{1,5},{5... | collective-permute-start | bytes 6291464 | tf_op jit(solution)/shard_map/ppermute | solution.py:79
  129.8 3.7 copy-start.15
  132.2 2.7 copy-start.25
  135.9 49.7 %collective-permute-start.6 = (bf16[1024,1024]{1,0:T(8,128)(2,1)}, bf16[1024,1024]{1,0:T(8,128)(2,1)S(1)}, u32[]{:S(2)}, u32[]{:S(2)}) collective-permute-start(bf16[1024,1024]{1,0:T(8,128)(2,1)} %collective-permute-done.5), channel_id=1, source_target_pairs={{4,0},{8,4},{12,8},{16,12},{20,16},{24,20},{28,24},{0,28},{5,1},{9... | collective-permute-start | bytes 6291464 | tf_op jit(solution)/shard_map/ppermute | solution.py:82
  221.9 15.2 %copy-start.23 = (bf16[640,512]{1,0:T(8,128)(2,1)S(1)}, bf16[640,512]{1,0:T(8,128)(2,1)}, u32[]{:S(2)}) copy-start(bf16[640,512]{1,0:T(8,128)(2,1)} %constant.59) | copy-start | bytes 1966084
  237.1 2.5 copy-start.22
  238.0 3.6 copy-start.27
  238.0 3.6 collective-permute-start.8
  246.5 5.4 %copy-start.21 = (bf16[640,512]{1,0:T(8,128)(2,1)S(1)}, bf16[640,512]{1,0:T(8,128)(2,1)}, u32[]{:S(2)}) copy-start(bf16[640,512]{1,0:T(8,128)(2,1)} %constant.51) | copy-start | bytes 1966084
  249.3 3.5 copy-start.20
  249.3 4.4 collective-permute-start.7
  277.1 184.0 %all-reduce.2.cloned.1.call-start = ((), (), s32[]{:S(2)}) async-start(), calls=%async_computation.2 | async-start | bytes 1048576 | tf_op jit(solution)/shard_map/psum | solution.py:112
  281.7 3.7 copy-start.7
  402.8 60.1 %copy-start.1 = (bf16[1024,128]{1,0:T(8,128)(2,1)S(1)}, bf16[1024,128]{1,0:T(8,128)(2,1)}, u32[]{:S(2)}) copy-start(bf16[1024,128]{1,0:T(8,128)(2,1)} %param.17) | copy-start | bytes 786436
  (18 other events, 29.4 us)
Sparse Core Ops, SparseCore 0:
  9.6 152.3 all-gather.1
  277.2 125.5 reduce-scatter.1
  406.5 54.5 all-reduce.1
